TPU v7x, 32 devices: a whole 2x2x4 slice. The times are simulated.
32 devices in a mesh: col: 8 (over z, x), tile: 4 (over y, core).
Axes of the slice: x: 2, y: 2, z: 4, core: 2. Of those that a mesh axis runs over, the one named last changes fastest.
Arguments:
- initial_image: float32 [16384, 1024], P('tile', 'col'), may hold values from -6 to 6
- panels: float32 [8, 256, 16384], P('col', None, 'tile'), may hold values from -0.046875 to 0.046875
- sinogram: float32 [8, 256, 1024], P(None, 'tile', 'col'), may hold values from -6 to 6
- subset_order: int32 [3], replicated, may hold values from 0 to 7
- step_sizes: float32 [3], replicated, may hold values from 0.5 to 1
Outputs:
- final_image: float32 [16384, 1024], P('tile', 'col')
- final_duals: float32 [8, 256, 1024], P(None, 'tile', 'col')
Inputs may be any that keep to these rules, and one draw needn't show every extreme that they name: `subset_order`: repeats may occur.
All inputs are finite; a program needn't handle non-finite values.
Results may differ from a plain program's by a relative error of at most 0.00013.
Values sent between devices are 32-bit elements; how exact they have to be, the bound alone decides.
No kernel may reach another device: no remote copies, remote signals or barrier semaphores. Data moves between devices by JAX's collectives and lax.ppermute only.
A program may use at most 128 MiB of HBM per device.

v0:
```python
import jax
import jax.numpy as jnp
from jax import lax
from jax.sharding import PartitionSpec as P

WIDTH = 512
ITERS = 3
penalty = 0.2
smoothing = 1.0


def shifted(value, axis, by):
    count = lax.axis_size(axis)
    pairs = [(i, i + by) for i in range(count) if 0 <= i + by < count]
    return lax.ppermute(value, axis, pairs)


def broadcast(value, axis, root):
    mine = lax.axis_index(axis) == root
    return lax.psum(jnp.where(mine, value, jnp.zeros_like(value)), axis)


def divergence(estimate, rows_local, tile_index, total_rows):
    channels = estimate.shape[1]
    image_field = estimate.reshape(rows_local, WIDTH, channels)
    row_below = shifted(image_field[0:1], "tile", -1)
    extended = jnp.concatenate([image_field, row_below], axis=0)
    downward = extended[1:] - extended[:-1]
    global_row = tile_index * rows_local + lax.broadcasted_iota(jnp.int32, (rows_local, 1, 1), 0)
    downward = jnp.where(global_row < total_rows - 1, downward, jnp.zeros_like(downward))
    column_zero = jnp.zeros((rows_local, 1, channels), estimate.dtype)
    across = jnp.concatenate([image_field[:, 1:] - image_field[:, :-1], column_zero], axis=1)
    magnitude = jnp.sqrt(across * across + downward * downward + smoothing * smoothing)
    flux_across = across / magnitude
    flux_down = downward / magnitude
    flux_above = shifted(flux_down[rows_local - 1 :], "tile", 1)
    shifted_across = jnp.concatenate([column_zero, flux_across[:, :-1]], axis=1)
    shifted_down = jnp.concatenate([flux_above, flux_down[:-1]], axis=0)
    divergence_field = flux_across - shifted_across + flux_down - shifted_down
    return divergence_field.reshape(estimate.shape)


def per_device(initial_image, panels, sinogram, subset_order, step_sizes):
    dual_step = step_sizes[0]
    primal_step = step_sizes[1]
    extrapolate = step_sizes[2]
    tile_count = lax.axis_size("tile")
    tile_index = lax.axis_index("tile")
    rows_local = initial_image.shape[0] // WIDTH
    total_rows = rows_local * tile_count
    stored = panels.shape[0]
    rays_local = panels.shape[1] // tile_count
    subset_count = sinogram.shape[0]

    def primal(estimate, extrapolated):
        field_div = divergence(estimate, rows_local, tile_index, total_rows)
        return estimate - primal_step * extrapolated + primal_step * penalty * field_div

    estimate = initial_image
    dual_state = jnp.zeros(sinogram.shape, jnp.float32)
    accumulated = jnp.zeros(initial_image.shape, jnp.float32)
    extrapolated = jnp.zeros(initial_image.shape, jnp.float32)
    for iteration in range(ITERS):
        estimate = primal(estimate, extrapolated)
        subset = subset_order[iteration]
        owner_index = subset // stored
        own_panel = lax.dynamic_index_in_dim(panels, subset % stored, 0, keepdims=False)
        operator_panel = broadcast(own_panel, "col", owner_index)
        current = lax.dynamic_index_in_dim(dual_state, subset, 0, keepdims=False)
        measured = lax.dynamic_index_in_dim(sinogram, subset, 0, keepdims=False)

        def partial_rows(first_row, row_count, operator_panel=operator_panel, estimate=estimate):
            return jnp.dot(
                operator_panel,
                estimate,
                precision=lax.Precision.HIGHEST,
                preferred_element_type=jnp.float32,
            )

        forward = lax.psum_scatter(
            partial_rows(jnp.int32(0), rays_local * lax.axis_size("tile")),
            "tile",
            scatter_dimension=0,
            tiled=True,
        )
        updated = (current + dual_step * forward - dual_step * measured) / (1.0 + dual_step)
        change = updated - current

        def add_back(running, received, first_row, operator_panel=operator_panel):
            return lax.dot_general(
                operator_panel,
                received,
                (((0,), (0,)), ((), ())),
                precision=lax.Precision.HIGHEST,
                preferred_element_type=jnp.float32,
            )

        adjoint = add_back(
            jnp.zeros(estimate.shape, jnp.float32),
            lax.all_gather(change, "tile", axis=0, tiled=True),
            jnp.int32(0),
        )
        dual_state = lax.dynamic_update_index_in_dim(dual_state, updated, subset, 0)
        accumulated = accumulated + adjoint
        extrapolated = accumulated + extrapolate * subset_count * adjoint
    final_image = primal(estimate, extrapolated)
    return (final_image, dual_state)


def solution(mesh):
    in_specs = (P("tile", "col"), P("col", None, "tile"), P(None, "tile", "col"), P(), P())
    out_specs = (P("tile", "col"), P(None, "tile", "col"))
    return jax.shard_map(
        per_device, mesh=mesh, in_specs=in_specs, out_specs=out_specs, check_vma=False
    )
```

profile of v0, /device:TPU:0, one launch (start us, length us, event | category | flops | bytes accessed | tf_op | source)
XLA Modules:
  0.0 561.9 jit_solution(9093737235696430673)
XLA Ops:
  7.2 1.4 fusion.30
  10.5 7.2 %select_bitcast_fusion = (f32[256,4096]{1,0:T(8,128)}, f32[256,4096]{1,0:T(8,128)}, f32[256,4096]{1,0:T(8,128)}) fusion(f32[1,256,4096]{2,1,0:T(8,128)} %param.6, pred[]{:T(512)S(6)} %eq.15, pred[]{:T(512)S(6)} %eq.13, pred[]{:T(512)S(6)} %eq.14), kind=kLoop, calls=%fused_computation | loop fusion | flops 3145728 | bytes 16777220 | tf_op jit(solution)/shard_map/jit(_where)/select_n | solution.py:20
  17.7 1.5 copy-done.4
  19.3 1.3 collective-permute-start
  20.8 1.9 collective-permute-done
  22.7 2.5 fusion.22
  25.2 1.4 copy-done.6
  26.6 8.1 %collective-permute-start.1 = (f32[1,512,128]{2,1,0:T(8,128)S(1)}, f32[1,512,128]{2,1,0:T(8,128)S(1)}, u32[]{:S(2)}, u32[]{:S(2)}) collective-permute-start(f32[1,512,128]{2,1,0:T(8,128)S(1)} %slice.155), channel_id=1, source_target_pairs={{0,1},{1,2},{2,3},{4,5},{5,6},{6,7},{8,9},{9,10},{10,11},{12,13},{... | collective-permute-start | bytes 786440 | tf_op jit(solution)/shard_map/ppermute | solution.py:15
  38.5 0.7 fusion.29
  43.6 1.6 slice.156
  45.2 2.9 fusion.11
  48.4 1.3 collective-permute-start.2
  49.9 1.9 collective-permute-done.2
  51.9 2.5 fusion.20
  54.4 1.5 slice.162
  56.2 6.6 %collective-permute-start.3 = (f32[1,512,128]{2,1,0:T(8,128)S(1)}, f32[1,512,128]{2,1,0:T(8,128)S(1)}, u32[]{:S(2)}, u32[]{:S(2)}) collective-permute-start(f32[1,512,128]{2,1,0:T(8,128)S(1)} %slice.161), channel_id=1, source_target_pairs={{0,1},{1,2},{2,3},{4,5},{5,6},{6,7},{8,9},{9,10},{10,11},{12,13},{... | collective-permute-start | bytes 786440 | tf_op jit(solution)/shard_map/ppermute | solution.py:15
  62.9 352.5 %all-reduce.11.cloned.1.call-done = (f32[256,4096]{1,0:T(8,128)}, f32[256,4096]{1,0:T(8,128)}, f32[256,4096]{1,0:T(8,128)}) async-done(((f32[256,4096]{1,0:T(8,128)}, f32[256,4096]{1,0:T(8,128)}, f32[256,4096]{1,0:T(8,128)}), (f32[256,4096]{1,0:T(8,128)}, f32[256,4096]{1,0:T(8,128)}, f32[256,4096]{1,0:T(8,128)})) %all-reduce.11.cloned.1.call-update) | async-done | bytes 12582928 | tf_op jit(solution)/shard_map/psum | solution.py:20
  415.4 5.9 %fusion.31 = f32[256,128]{1,0:T(8,128)} fusion(f32[256,4096]{1,0:T(8,128)} %get-tuple-element.2, f32[4096,128]{1,0:T(8,128)S(1)} %bitcast_add_fusion.2), kind=kOutput, calls=%fused_computation.66 | convolution fusion | flops 1610612736 | bytes 6422528 | tf_op jit(solution)/shard_map/dot_general | solution.py:73
  421.3 5.1 fusion.12
  426.5 13.7 %reduce-scatter.4.cloned.1.call-done = f32[64,128]{1,0:T(8,128)} async-done(((f32[256,128]{1,0:T(8,128)}), f32[64,128]{1,0:T(8,128)}) %reduce-scatter.4.cloned.1.call-update) | async-done | bytes 32784 | tf_op jit(solution)/shard_map/reduce_scatter | solution.py:80
  440.2 1.3 bitcast_dynamic-update-slice_fusion.2
  441.5 5.9 %all_gather.9 = f32[256,128]{1,0:T(8,128)S(1)} all-gather(f32[64,128]{1,0:T(8,128)S(1)} %get-tuple-element.12), channel_id=1, replica_groups=mesh['col'=8,'tile'=4] {'tile'}, dimensions={0}, use_global_device_ids=true | all-gather | bytes 163840 | tf_op jit(solution)/shard_map/all_gather | solution.py:100
  447.4 11.9 %fusion.2 = (f32[4096,128]{1,0:T(8,128)S(1)}, f32[4096,128]{1,0:T(8,128)}) fusion(f32[4096,128]{1,0:T(8,128)S(1)} %bitcast_add_fusion.2, f32[8,512,128]{2,1,0:T(8,128)} %fusion.12, f32[]{:T(128)} %bitcast.8, f32[]{:T(128)} %bitcast, f32[256,4096]{1,0:T(8,128)} %get-tuple-element.2, f32[256,128]{1,0:T(8,128)S(1)} %all_gather.9), kind=kOutput, calls=%fused_computation.6 | convolution fusion | flops 1613234176 | bytes 12713992 | tf_op jit(solution)/shard_map/dot_general | solution.py:90
  459.3 1.3 copy-done
  460.6 4.1 fusion.32
  464.8 1.3 collective-permute-start.4
  466.1 2.6 slice_subtract_fusion.1
  469.0 2.5 fusion.18
  471.5 1.5 slice.168
  473.4 5.8 %collective-permute-start.5 = (f32[1,512,128]{2,1,0:T(8,128)S(1)}, f32[1,512,128]{2,1,0:T(8,128)S(1)}, u32[]{:S(2)}, u32[]{:S(2)}) collective-permute-start(f32[1,512,128]{2,1,0:T(8,128)S(1)} %slice.167), channel_id=1, source_target_pairs={{0,1},{1,2},{2,3},{4,5},{5,6},{6,7},{8,9},{9,10},{10,11},{12,13},{... | collective-permute-start | bytes 786440 | tf_op jit(solution)/shard_map/ppermute | solution.py:15
  479.2 5.4 reduce-scatter.6.cloned.1.call-done
  484.6 1.3 bitcast_subtract_fusion.3
  485.9 5.6 all_gather.10
  491.5 4.0 fusion.13
  496.1 0.7 copy-done.14
  496.8 9.3 %bitcast_add_fusion.1 = (f32[4096,128]{1,0:T(8,128)S(1)}, f32[4096,128]{1,0:T(8,128)}) fusion(f32[8,512,128]{2,1,0:T(8,128)S(1)} %fusion.13, f32[4096,128]{1,0:T(8,128)S(1)} %copy-done.1, f32[]{:T(128)} %bitcast.8, f32[]{:T(128)} %bitcast, f32[4096,128]{1,0:T(8,128)S(1)} %copy-done.14, f32[256,4096]{1,0:T(8,128)S(1)} %copy-done.13, ...), kind=kOutput, calls=%fused_computation.32 | convolution fusion | flops 1613758464 | bytes 14811144 | tf_op jit(solution)/shard_map/dot_general | solution.py:90
  506.1 1.4 copy-done.2
  507.5 4.1 fusion.33
  511.6 1.3 collective-permute-start.6
  512.9 4.0 slice_subtract_fusion
  516.9 14.6 %reduce-scatter.8.cloned.1.call-done = f32[64,128]{1,0:T(8,128)} async-done(((f32[256,128]{1,0:T(8,128)}), f32[64,128]{1,0:T(8,128)}) %reduce-scatter.8.cloned.1.call-update) | async-done | bytes 32784 | tf_op jit(solution)/shard_map/reduce_scatter | solution.py:80
  531.5 1.3 bitcast_subtract_fusion.1
  532.8 5.6 %all_gather.11 = f32[256,128]{1,0:T(8,128)S(1)} all-gather(f32[64,128]{1,0:T(8,128)S(1)} %get-tuple-element.5), channel_id=1, replica_groups=mesh['col'=8,'tile'=4] {'tile'}, dimensions={0}, use_global_device_ids=true | all-gather | bytes 163840 | tf_op jit(solution)/shard_map/all_gather | solution.py:100
  538.5 2.9 fusion.16
  541.4 2.3 collective-permute-start.7
  543.7 7.1 %fusion.34 = f32[4096,128]{1,0:T(8,128)S(1)} fusion(f32[256,4096]{1,0:T(8,128)S(1)} %copy-done.11, f32[256,128]{1,0:T(8,128)S(1)} %all_gather.11), kind=kOutput, calls=%fused_computation.69 | convolution fusion | flops 1610612736 | bytes 6422528 | tf_op jit(solution)/shard_map/dot_general | solution.py:90
  551.6 1.0 copy-done.15
  552.6 2.5 bitcast_add_fusion
  (61 shorter events, 3.6 us)
Async XLA Ops:
  7.2 408.2 %all-reduce.11.cloned.1.call-start = ((), (), s32[]{:S(2)}) async-start(), calls=%async_computation.6 | async-start | bytes 25165824 | tf_op jit(solution)/shard_map/psum | solution.py:20
  17.7 1.6 copy-start.4
  17.7 422.5 %reduce-scatter.4.cloned.1.call-start = ((), (), s32[]{:S(2)}) async-start(), calls=%async_computation.3 | async-start | bytes 163840 | tf_op jit(solution)/shard_map/reduce_scatter | solution.py:80
  19.3 3.4 collective-permute-start
  20.8 17.7 %copy-start.17 = (f32[3]{0:T(128)S(1)}, f32[3]{0:T(128)}, u32[]{:S(2)}) copy-start(f32[3]{0:T(128)} %param.9) | copy-start | bytes 40
  25.2 1.4 copy-start.6
  26.6 18.6 %copy-start.7 = (f32[8,512,128]{2,1,0:T(8,128)S(1)}, f32[8,512,128]{2,1,0:T(8,128)}, u32[]{:S(2)}) copy-start(f32[8,512,128]{2,1,0:T(8,128)} %copy-done.6) | copy-start | bytes 6291460
  26.6 18.6 %collective-permute-start.1 = (f32[1,512,128]{2,1,0:T(8,128)S(1)}, f32[1,512,128]{2,1,0:T(8,128)S(1)}, u32[]{:S(2)}, u32[]{:S(2)}) collective-permute-start(f32[1,512,128]{2,1,0:T(8,128)S(1)} %slice.155), channel_id=1, source_target_pairs={{0,1},{1,2},{2,3},{4,5},{5,6},{6,7},{8,9},{9,10},{10,11},{12,13},{... | collective-permute-start | bytes 786440 | tf_op jit(solution)/shard_map/ppermute | solution.py:15
  45.2 3.0 copy-start.5
  48.4 3.4 collective-permute-start.2
  54.3 1.9 copy-start.8
  56.2 365.1 %collective-permute-start.3 = (f32[1,512,128]{2,1,0:T(8,128)S(1)}, f32[1,512,128]{2,1,0:T(8,128)S(1)}, u32[]{:S(2)}, u32[]{:S(2)}) collective-permute-start(f32[1,512,128]{2,1,0:T(8,128)S(1)} %slice.161), channel_id=1, source_target_pairs={{0,1},{1,2},{2,3},{4,5},{5,6},{6,7},{8,9},{9,10},{10,11},{12,13},{... | collective-permute-start | bytes 786440 | tf_op jit(solution)/shard_map/ppermute | solution.py:15
  421.3 63.3 %reduce-scatter.6.cloned.1.call-start = ((), (), s32[]{:S(2)}) async-start(), calls=%async_computation.4 | async-start | bytes 163840 | tf_op jit(solution)/shard_map/reduce_scatter | solution.py:80
  447.4 13.2 %copy-start.12 = (f32[256,4096]{1,0:T(8,128)S(1)}, f32[256,4096]{1,0:T(8,128)}, u32[]{:S(2)}) copy-start(f32[256,4096]{1,0:T(8,128)} %get-tuple-element.3) | copy-start | bytes 12582916
  459.3 1.3 copy-start
  464.8 66.7 %reduce-scatter.8.cloned.1.call-start = ((), (), s32[]{:S(2)}) async-start(), calls=%async_computation.5 | async-start | bytes 163840 | tf_op jit(solution)/shard_map/reduce_scatter | solution.py:80
  464.8 3.9 collective-permute-start.4
  466.1 2.9 copy-start.1
  471.5 1.9 copy-start.9
  473.4 18.1 %collective-permute-start.5 = (f32[1,512,128]{2,1,0:T(8,128)S(1)}, f32[1,512,128]{2,1,0:T(8,128)S(1)}, u32[]{:S(2)}, u32[]{:S(2)}) collective-permute-start(f32[1,512,128]{2,1,0:T(8,128)S(1)} %slice.167), channel_id=1, source_target_pairs={{0,1},{1,2},{2,3},{4,5},{5,6},{6,7},{8,9},{9,10},{10,11},{12,13},{... | collective-permute-start | bytes 786440 | tf_op jit(solution)/shard_map/ppermute | solution.py:15
  491.5 4.6 copy-start.13
  491.5 5.3 copy-start.14
  496.8 10.7 %copy-start.10 = (f32[256,4096]{1,0:T(8,128)S(1)}, f32[256,4096]{1,0:T(8,128)}, u32[]{:S(2)}) copy-start(f32[256,4096]{1,0:T(8,128)} %get-tuple-element.4) | copy-start | bytes 12582916
  506.1 1.4 copy-start.2
  511.6 26.8 %collective-permute-start.6 = (f32[1,512,128]{2,1,0:T(8,128)S(1)}, f32[1,512,128]{2,1,0:T(8,128)S(1)}, u32[]{:S(2)}, u32[]{:S(2)}) collective-permute-start(f32[1,512,128]{2,1,0:T(8,128)S(1)} %slice_bitcast_fusion), channel_id=1, source_target_pairs={{1,0},{2,1},{3,2},{5,4},{6,5},{7,6},{9,8},{10,9},{11,10},{13,12},{... | collective-permute-start | bytes 786440 | tf_op jit(solution)/shard_map/ppermute | solution.py:15
  512.9 25.5 %copy-start.3 = (f32[4096,128]{1,0:T(8,128)S(1)}, f32[4096,128]{1,0:T(8,128)}, u32[]{:S(2)}) copy-start(f32[4096,128]{1,0:T(8,128)} %copy-done.2) | copy-start | bytes 6291460
  538.5 5.2 copy-start.11
  541.4 9.5 %collective-permute-start.7 = (f32[1,512,128]{2,1,0:T(8,128)S(1)}, f32[1,512,128]{2,1,0:T(8,128)S(1)}, u32[]{:S(2)}, u32[]{:S(2)}) collective-permute-start(f32[1,512,128]{2,1,0:T(8,128)S(1)} %slice.173), channel_id=1, source_target_pairs={{0,1},{1,2},{2,3},{4,5},{5,6},{6,7},{8,9},{9,10},{10,11},{12,13},{... | collective-permute-start | bytes 786440 | tf_op jit(solution)/shard_map/ppermute | solution.py:15
  550.9 0.7 copy-start.16
  550.9 1.7 copy-start.15
Sparse Core Ops, SparseCore 0:
  17.8 397.5 all-reduce.10
  421.4 18.7 reduce-scatter.3
  464.9 19.6 reduce-scatter.5
  511.7 19.6 reduce-scatter.7
where the time goes:
time: 569 us; the launch traced here: 562 us
  waiting for transfers between devices  390 us (69%)
  other arithmetic  43.8 us (8%)
  matrix products  42.4 us (7%)
  starting transfers between devices  28 us (5%)
  between operations  24.4 us (4%)
  blocking collectives  17.1 us (3%)
  local copies, waits for them, and re-layouts  16.1 us (3%)
    psum x1, waiting for transfers between devices, broadcast(): return lax.psum(jnp.where(mine, value, jnp.zeros_like(value)), axis)  352 us
    reduce_scatter x3, waiting for transfers between devices, per_device(): lax.psum_scatter(partial_rows(jnp.int32(0), rays_local * lax.axis_size('t...  33.7 us
    dot_general x3, matrix products, add_back(): lax.dot_general(operator_panel, received, (((0,), (0,)), ((), ())), preci...  28.2 us
    ppermute x8, starting transfers between devices, shifted(): return lax.ppermute(value, axis, pairs)  27.9 us
    all_gather x3, blocking collectives, per_device(): lax.all_gather(change, 'tile', axis=0, tiled=True)  17.1 us
    dot_general x3, matrix products, partial_rows(): jnp.dot(operator_panel, estimate, precision=lax.Precision.HIGHEST, prefer...  14.1 us
    mul x4, other arithmetic, primal(): primal_step * penalty * field_div  12.5 us
  transfers between devices with their start and end apart: 12, of which 6 were waited for; matrix products, arithmetic and copies ran while one was open for 8% of the time, Pallas kernels for 0%

commit v1 on v0

--- a/solution.py
+++ b/solution.py
@@ -17,7 +17,7 @@
 
 def broadcast(value, axis, root):
     mine = lax.axis_index(axis) == root
-    return lax.psum(jnp.where(mine, value, jnp.zeros_like(value)), axis)
+    return jnp.sum(lax.all_gather(jnp.where(mine, value, jnp.zeros_like(value)), axis), axis=0)
 
 
 def divergence(estimate, rows_local, tile_index, total_rows):

time: 569 us -> 2090 us (3.67)
  waiting for transfers between devices: 390 us -> 1870 us
  other arithmetic: 43.8 us -> 87.8 us
    all_gather x0 -> x3, waiting for transfers between devices: none -> 1830 us  [broadcast(): lax.all_gather(jnp.where(mine, value, jnp.zeros_like(value)), axis)]
    psum x1 -> x0, waiting for transfers between devices: 352 us -> none  [broadcast(): return lax.psum(jnp.where(mine, value, jnp.zeros_like(value)), axis)]
    reduce_sum x0 -> x3, other arithmetic: none -> 43.8 us  [broadcast(): jnp.sum(lax.all_gather(jnp.where(mine, value, jnp.zeros_like(value)), axi...]
  transfers between devices with their start and end apart: 12 -> 14, of which waited for: 6 -> 8; matrix products, arithmetic and copies ran while one was open for 8% -> 4% of each run, Pallas kernels for 0% -> 0%
where the time goes in v1:
time: 2090 us; the launch traced here: 2080 us
  waiting for transfers between devices  1870 us (89%)
  other arithmetic  87.8 us (4%)
  matrix products  42.1 us (2%)
  starting transfers between devices  28.1 us (1%)
  between operations  24.5 us (1%)
    all_gather x3, waiting for transfers between devices, broadcast(): lax.all_gather(jnp.where(mine, value, jnp.zeros_like(value)), axis)  1830 us
    reduce_sum x3, other arithmetic, broadcast(): jnp.sum(lax.all_gather(jnp.where(mine, value, jnp.zeros_like(value)), axi...  43.8 us
  transfers between devices with their start and end apart: 14, of which 8 were waited for; matrix products, arithmetic and copies ran while one was open for 4% of the time, Pallas kernels for 0%

profile of v1, /device:TPU:0, one launch (start us, length us, event | category | flops | bytes accessed | tf_op | source)
XLA Modules:
  0.0 2081.1 jit_solution(12999687777444915782)
XLA Ops:
  7.2 1.4 fusion.29
  10.4 7.2 broadcast_select_fusion
  20.1 1.3 collective-permute-start
  21.6 1.9 collective-permute-done
  23.5 2.5 fusion.22
  26.0 1.4 copy-done.10
  27.4 8.1 collective-permute-start.1
  44.2 1.6 slice.156
  45.9 2.9 fusion.11
  49.0 1.3 collective-permute-start.2
  50.5 1.9 collective-permute-done.2
  52.5 2.5 fusion.20
  55.0 1.4 slice.162
  56.9 6.6 collective-permute-start.3
  63.4 594.8 %all-gather.4.cloned.1.call-done = f32[8,256,4096]{2,1,0:T(8,128)} async-done(((f32[1,256,4096]{2,1,0:T(8,128)}), f32[8,256,4096]{2,1,0:T(8,128)}) %all-gather.4.cloned.1.call-update) | async-done | bytes 33554448 | tf_op jit(solution)/shard_map/all_gather | solution.py:20
  658.2 14.8 reduce_sum.27
  673.0 5.9 fusion.31
  679.0 5.1 fusion.12
  684.1 613.3 %all-gather.6.cloned.1.call-done = f32[8,256,4096]{2,1,0:T(8,128)} async-done(((f32[1,256,4096]{2,1,0:T(8,128)}), f32[8,256,4096]{2,1,0:T(8,128)}) %all-gather.6.cloned.1.call-update) | async-done | bytes 33554448 | tf_op jit(solution)/shard_map/all_gather | solution.py:20
  1297.4 14.9 reduce_sum.28
  1312.3 624.4 %all-gather.8.cloned.1.call-done = f32[8,256,4096]{2,1,0:T(8,128)} async-done(((f32[1,256,4096]{2,1,0:T(8,128)}), f32[8,256,4096]{2,1,0:T(8,128)}) %all-gather.8.cloned.1.call-update) | async-done | bytes 33554448 | tf_op jit(solution)/shard_map/all_gather | solution.py:20
  1936.6 14.1 reduce_sum.29
  1950.7 8.4 reduce-scatter.4.cloned.1.call-done
  1959.1 1.5 bitcast_dynamic-update-slice_fusion.2
  1960.6 5.9 all_gather.22
  1966.5 11.7 fusion.2
  1978.2 1.3 copy-done
  1979.5 4.1 fusion.32
  1983.7 1.3 collective-permute-start.4
  1985.0 2.6 slice_subtract_fusion.1
  1987.8 2.5 fusion.18
  1990.3 1.5 slice.168
  1992.3 5.8 collective-permute-start.5
  1998.1 5.3 reduce-scatter.6.cloned.1.call-done
  2003.4 1.5 bitcast_subtract_fusion.3
  2004.9 5.6 all_gather.24
  2010.5 4.0 fusion.13
  2015.7 9.2 bitcast_add_fusion.1
  2025.0 1.3 copy-done.2
  2026.3 4.1 fusion.33
  2031.8 3.9 slice_subtract_fusion
  2035.7 14.6 reduce-scatter.8.cloned.1.call-done
  2050.3 1.5 bitcast_subtract_fusion.1
  2051.8 5.6 all_gather.26
  2057.4 2.9 fusion.16
  2060.4 2.3 collective-permute-start.7
  2062.7 7.1 fusion.34
  2071.6 2.4 bitcast_add_fusion
  (70 shorter events, 9.6 us)
Async XLA Ops:
  7.2 651.0 %all-gather.4.cloned.1.call-start = ((), (), s32[]{:S(2)}) async-start(), calls=%async_computation.3 | async-start | bytes 37748736 | tf_op jit(solution)/shard_map/all_gather | solution.py:20
  17.7 1279.7 %all-gather.6.cloned.1.call-start = ((), (), s32[]{:S(2)}) async-start(), calls=%async_computation.5 | async-start | bytes 37748736 | tf_op jit(solution)/shard_map/all_gather | solution.py:20
  18.4 1918.2 %all-gather.8.cloned.1.call-start = ((), (), s32[]{:S(2)}) async-start(), calls=%async_computation.7 | async-start | bytes 37748736 | tf_op jit(solution)/shard_map/all_gather | solution.py:20
  18.5 1.6 copy-start.8
  19.2 1939.9 %reduce-scatter.4.cloned.1.call-start = ((), (), s32[]{:S(2)}) async-start(), calls=%async_computation.4 | async-start | bytes 163840 | tf_op jit(solution)/shard_map/reduce_scatter | solution.py:80
  20.1 3.4 collective-permute-start
  21.6 17.6 copy-start.17
  26.0 1.4 copy-start.10
  27.4 18.4 copy-start.11
  27.4 18.4 collective-permute-start.1
  45.8 2.9 copy-start.9
  49.0 3.4 collective-permute-start.2
  54.9 1.9 copy-start.12
  56.9 622.1 %collective-permute-start.3 = (f32[1,512,128]{2,1,0:T(8,128)S(1)}, f32[1,512,128]{2,1,0:T(8,128)S(1)}, u32[]{:S(2)}, u32[]{:S(2)}) collective-permute-start(f32[1,512,128]{2,1,0:T(8,128)S(1)} %slice.161), channel_id=1, source_target_pairs={{0,1},{1,2},{2,3},{4,5},{5,6},{6,7},{8,9},{9,10},{10,11},{12,13},{... | collective-permute-start | bytes 786440 | tf_op jit(solution)/shard_map/ppermute | solution.py:15
  678.9 1324.5 %reduce-scatter.6.cloned.1.call-start = ((), (), s32[]{:S(2)}) async-start(), calls=%async_computation.6 | async-start | bytes 163840 | tf_op jit(solution)/shard_map/reduce_scatter | solution.py:80
  1966.5 13.0 copy-start.6
  1978.2 1.3 copy-start
  1983.6 66.7 %reduce-scatter.8.cloned.1.call-start = ((), (), s32[]{:S(2)}) async-start(), calls=%async_computation.8 | async-start | bytes 163840 | tf_op jit(solution)/shard_map/reduce_scatter | solution.py:80
  1983.7 3.9 collective-permute-start.4
  1985.0 2.9 copy-start.1
  1990.3 1.9 copy-start.13
  1992.3 18.2 collective-permute-start.5
  2010.5 4.6 copy-start.7
  2010.5 5.3 copy-start.14
  2015.7 10.6 copy-start.4
  2025.0 1.4 copy-start.2
  2030.5 27.0 %collective-permute-start.6 = (f32[1,512,128]{2,1,0:T(8,128)S(1)}, f32[1,512,128]{2,1,0:T(8,128)S(1)}, u32[]{:S(2)}, u32[]{:S(2)}) collective-permute-start(f32[1,512,128]{2,1,0:T(8,128)S(1)} %slice_bitcast_fusion), channel_id=1, source_target_pairs={{1,0},{2,1},{3,2},{5,4},{6,5},{7,6},{9,8},{10,9},{11,10},{13,12},{... | collective-permute-start | bytes 786440 | tf_op jit(solution)/shard_map/ppermute | solution.py:15
  2031.8 25.7 %copy-start.3 = (f32[4096,128]{1,0:T(8,128)S(1)}, f32[4096,128]{1,0:T(8,128)}, u32[]{:S(2)}) copy-start(f32[4096,128]{1,0:T(8,128)} %copy-done.2) | copy-start | bytes 6291460
  2057.4 5.2 copy-start.5
  2060.4 9.5 collective-permute-start.7
  2069.9 0.7 copy-start.16
  2069.9 1.7 copy-start.15
Sparse Core Ops, SparseCore 0:
  17.8 640.3 all-gather.3
  659.7 637.6 all-gather.5
  1298.9 637.6 all-gather.7
  1939.5 19.5 reduce-scatter.3
  1983.8 19.6 reduce-scatter.5
  2030.6 19.6 reduce-scatter.7
